TPU v7x, 32 devices: a whole 2x2x4 slice. The times are simulated.
32 devices in a mesh: seq: 8 (over z, x), fsdp: 4 (over y, core).
Axes of the slice: x: 2, y: 2, z: 4, core: 2. Of those that a mesh axis runs over, the one named last changes fastest.
Arguments:
- tokens: bfloat16 [4, 2048, 1536], P('fsdp', 'seq'), may hold values from -6 to 6
- lengths: int32 [4], P('fsdp'), may hold values from 512 to 2048, as said below
- norm_gain: bfloat16 [1536], P('fsdp'), may hold values from 0.099609375 to 1.8984375
- in_weight: bfloat16 [1536, 6448], P('fsdp'), may hold values from -0.15625 to 0.15625
- conv_weight: bfloat16 [4, 3328], P(None, 'fsdp'), may hold values from -3 to 3
- conv_bias: bfloat16 [3328], P('fsdp'), may hold values from -0.5 to 0.5
- dt_bias: bfloat16 [48], P('fsdp'), may hold values from -4.5 to -3.5
- decay_log: bfloat16 [48], P('fsdp'), may hold values from -9 to 0
- skip_gain: bfloat16 [48], P('fsdp'), may hold values from 0.5 to 1.5
- gated_gain: bfloat16 [3072], P('fsdp'), may hold values from 0.099609375 to 1.8984375
- out_weight: bfloat16 [3072, 1536], P('fsdp'), may hold values from -0.109375 to 0.109375
- cotangent: bfloat16 [4, 2048, 1536], P('fsdp', 'seq'), may hold values from -6 to 6
Outputs:
- mixed: bfloat16 [4, 2048, 1536], P('fsdp', 'seq')
- input_grad: float32 [4, 2048, 1536], P('fsdp', 'seq')
- norm_gain_grad: float32 [1536], P('fsdp')
- in_weight_grad: float32 [1536, 6448], P('fsdp')
- conv_weight_grad: float32 [4, 3328], P(None, 'fsdp')
- conv_bias_grad: float32 [3328], P('fsdp')
- dt_bias_grad: float32 [48], P('fsdp')
- decay_log_grad: float32 [48], P('fsdp')
- skip_gain_grad: float32 [48], P('fsdp')
- gated_gain_grad: float32 [3072], P('fsdp')
- out_weight_grad: float32 [3072, 1536], P('fsdp')
Inputs may be any that keep to these rules, and one draw needn't show every extreme that they name: `lengths`: each slot's valid positions come first; some slot has all 2048 valid.
All inputs are finite; a program needn't handle non-finite values.
Results may differ from a plain program's by a relative error of at most 0.012.
The roundings to bfloat16 on the way count: a program that leaves them out, or rounds other values in their place, can miss the bound.
Values may be sent and summed in bfloat16 or wider, within the bound.
No kernel may reach another device: no remote copies, remote signals or barrier semaphores. Data moves between devices by JAX's collectives and lax.ppermute only.
A program may use at most 256 MiB of HBM per device.

v0:
```python
import jax
import jax.numpy as jnp
from jax import lax
from jax.sharding import PartitionSpec as P

epsilon = 1e-05
triple = lax.Precision.HIGH


def from_behind(value, axis, by):
    count = lax.axis_size(axis)
    pairs = [(i, i + by) for i in range(count) if 0 <= i + by < count]
    return lax.ppermute(value, axis, pairs)


def carried_in(value, axis, combine, identity, reverse):
    count, position = (lax.axis_size(axis), lax.axis_index(axis))
    everything = jax.tree.map(lambda part: lax.all_gather(part, axis), value)
    start = jax.tree.map(
        lambda part, zero: jnp.broadcast_to(jnp.asarray(zero, part.dtype), part.shape),
        value,
        identity,
    )

    def lap(k, before):
        at = count - 1 - k if reverse else k
        reached = at > position if reverse else at < position
        new = combine(before, jax.tree.map(lambda part: part[at], everything))
        return jax.tree.map(lambda a, b: jnp.where(reached, a, b), new, before)

    return lax.fori_loop(0, count, lap, start)


def rms_scale(inputs, gain):
    inv_rms = lax.rsqrt(jnp.mean(inputs * inputs, axis=-1, keepdims=True) + epsilon)
    return inputs * inv_rms * gain


def convolve(extended, conv_w, conv_b):
    taps = conv_w.shape[0]
    count = extended.shape[1] - taps + 1
    summed = conv_b + jnp.zeros(extended[:, :count].shape, jnp.float32)
    for offset in range(taps):
        summed = summed + extended[:, offset : offset + count] * conv_w[offset]
    return jax.nn.silu(summed)


def local_scan(values, b_rows, c_rows, step_raw, dt_b, decay_l):
    step_size = jax.nn.softplus(step_raw + dt_b)
    log_decay = jnp.cumsum(-step_size * jnp.exp(decay_l), axis=1)
    count = values.shape[1]
    places = jnp.arange(count)
    lower = (places[:, None] >= places[None, :])[None, :, :, None]
    gaps = log_decay[:, :, None, :] - log_decay[:, None, :, :]
    weights = jnp.where(lower, jnp.exp(jnp.where(lower, gaps, 0.0)), 0.0)
    intersection = jnp.einsum("stn,sun->stu", c_rows, b_rows, precision=triple)
    mixing = weights * intersection[..., None] * step_size[:, None, :, :]
    local_out = jnp.einsum("stuh,suhp->sthp", mixing, values, precision=triple)
    to_end = jnp.exp(log_decay[:, -1:, :] - log_decay) * step_size
    local_state = jnp.einsum("sqh,sqhp,sqn->shpn", to_end, values, b_rows, precision=triple)
    return (local_out, local_state, jnp.exp(log_decay[:, -1, :]), jnp.exp(log_decay))


def finish(local_out, c_rows, decay_in, state_in, values, skip_g, gate_part, gated_g):
    carried_out = decay_in[..., None] * jnp.einsum(
        "sqn,shpn->sqhp", c_rows, state_in, precision=triple
    )
    mixed_heads = local_out + carried_out + skip_g[:, None] * values
    flat = mixed_heads.reshape(gate_part.shape)
    return rms_scale(flat * jax.nn.silu(gate_part), gated_g)


def chain(earlier, later):
    return (earlier[0] * later[0], later[0][..., None, None] * earlier[1] + later[1])


def per_device(
    tokens,
    lengths,
    norm_gain,
    in_weight,
    conv_weight,
    conv_bias,
    dt_bias,
    decay_log,
    skip_gain,
    gated_gain,
    out_weight,
    cotangent,
):
    gathered = (
        lax.all_gather(norm_gain, "fsdp", axis=0, tiled=True),
        lax.all_gather(in_weight, "fsdp", axis=0, tiled=True),
        lax.all_gather(conv_weight, "fsdp", axis=1, tiled=True),
        lax.all_gather(conv_bias, "fsdp", axis=0, tiled=True),
        lax.all_gather(dt_bias, "fsdp", axis=0, tiled=True),
        lax.all_gather(decay_log, "fsdp", axis=0, tiled=True),
        lax.all_gather(skip_gain, "fsdp", axis=0, tiled=True),
        lax.all_gather(gated_gain, "fsdp", axis=0, tiled=True),
        lax.all_gather(out_weight, "fsdp", axis=0, tiled=True),
    )
    full_in = gathered[1]
    full_out = gathered[8]
    norm_f, conv_wf, conv_bf, dtb_f, decay_f, skip_f, ggain_f = [
        gathered[index].astype(jnp.float32) for index in (0, 2, 3, 4, 5, 6, 7)
    ]
    slots, seg, width = tokens.shape
    inner = full_out.shape[0]
    heads = dtb_f.shape[0]
    head_size = inner // heads
    conv_width = conv_wf.shape[1]
    state_width = (conv_width - inner) // 2
    taps = conv_wf.shape[0]
    places = lax.axis_index("seq") * seg + jnp.arange(seg)
    valid = (places[None, :] < lengths[:, None]).astype(jnp.float32)
    inputs = tokens.astype(jnp.float32)
    normed_f, pull_norm = jax.vjp(rms_scale, inputs, norm_f)
    normed = normed_f.astype(jnp.bfloat16)
    projected = jnp.einsum(
        "sqd,dp->sqp", normed, full_in, preferred_element_type=jnp.float32
    ).astype(jnp.bfloat16)
    gate_part = projected[..., :inner].astype(jnp.float32)
    conv_in = projected[..., inner : inner + conv_width]
    step_raw = projected[..., inner + conv_width :].astype(jnp.float32)
    previous = from_behind(conv_in[:, seg - (taps - 1) :], "seq", 1)
    extended = jnp.concatenate([previous, conv_in], axis=1).astype(jnp.float32)
    activated_f, pull_conv = jax.vjp(convolve, extended, conv_wf, conv_bf)
    activated = lax.optimization_barrier(activated_f.astype(jnp.bfloat16)).astype(jnp.float32)
    values = activated[..., :inner].reshape(slots, seg, heads, head_size)
    b_rows = activated[..., inner : inner + state_width]
    c_rows = activated[..., inner + state_width :]
    scanned, pull_local = jax.vjp(local_scan, values, b_rows, c_rows, step_raw, dtb_f, decay_f)
    local_out, local_state, whole_decay, decay_in = scanned
    identity = (
        jnp.ones((slots, heads), jnp.float32),
        jnp.zeros((slots, heads, head_size, state_width), jnp.float32),
    )
    state_in = carried_in((whole_decay, local_state), "seq", chain, identity, False)[1]
    gated_f, pull_finish = jax.vjp(
        finish, local_out, c_rows, decay_in, state_in, values, skip_f, gate_part, ggain_f
    )
    gated_out = gated_f.astype(jnp.bfloat16)
    branch = jnp.einsum("sqi,id->sqd", gated_out, full_out, preferred_element_type=jnp.float32)
    mixed = (valid[..., None] * (inputs + branch)).astype(jnp.bfloat16)
    back_in, back_out = (
        lax.all_gather(in_weight, "fsdp", axis=0, tiled=True),
        lax.all_gather(out_weight, "fsdp", axis=0, tiled=True),
    )
    upstream = valid[..., None] * cotangent.astype(jnp.float32)
    back_branch = upstream.astype(jnp.bfloat16)
    grad_out_w = jnp.einsum(
        "sqi,sqd->id", gated_out, back_branch, preferred_element_type=jnp.float32
    )
    back_gated = jnp.einsum(
        "sqd,id->sqi", back_branch, back_out, preferred_element_type=jnp.float32
    )
    d_local, d_crows_one, d_decay_in, d_state_local, d_values_one, d_skip, d_gate, d_ggain = (
        pull_finish(back_gated)
    )
    state_after = carried_in((whole_decay, d_state_local), "seq", chain, identity, True)[1]
    d_whole = jnp.sum(state_after * state_in, axis=(2, 3))
    d_values_two, d_brows, d_crows_two, d_step, d_dtb, d_decay = pull_local(
        (d_local, state_after, d_whole, d_decay_in)
    )
    d_active = jnp.concatenate(
        [
            (d_values_one + d_values_two).reshape(slots, seg, inner),
            d_brows,
            d_crows_one + d_crows_two,
        ],
        axis=-1,
    )
    d_extended, d_conv_w, d_conv_b = pull_conv(d_active)
    returned = from_behind(d_extended[:, : taps - 1].astype(jnp.bfloat16), "seq", -1).astype(
        jnp.float32
    )
    d_conv_in = d_extended[:, taps - 1 :] + jnp.pad(returned, ((0, 0), (seg - taps + 1, 0), (0, 0)))
    back_projected = jnp.concatenate([d_gate, d_conv_in, d_step], axis=-1).astype(jnp.bfloat16)
    grad_in_w = jnp.einsum(
        "sqd,sqp->dp", normed, back_projected, preferred_element_type=jnp.float32
    )
    back_normed = jnp.einsum(
        "sqp,dp->sqd", back_projected, back_in, preferred_element_type=jnp.float32
    )
    d_inputs, d_norm = pull_norm(back_normed)
    input_grad = upstream + d_inputs
    shares = (
        lax.psum_scatter(d_norm, "fsdp", scatter_dimension=0, tiled=True),
        lax.psum_scatter(grad_in_w, "fsdp", scatter_dimension=0, tiled=True),
        lax.psum_scatter(d_conv_w, "fsdp", scatter_dimension=1, tiled=True),
        lax.psum_scatter(d_conv_b, "fsdp", scatter_dimension=0, tiled=True),
        lax.psum_scatter(d_dtb, "fsdp", scatter_dimension=0, tiled=True),
        lax.psum_scatter(d_decay, "fsdp", scatter_dimension=0, tiled=True),
        lax.psum_scatter(d_skip, "fsdp", scatter_dimension=0, tiled=True),
        lax.psum_scatter(d_ggain, "fsdp", scatter_dimension=0, tiled=True),
        lax.psum_scatter(grad_out_w, "fsdp", scatter_dimension=0, tiled=True),
    )
    totals = lax.psum(
        (
            shares[0],
            shares[1],
            shares[2],
            shares[3],
            shares[4],
            shares[5],
            shares[6],
            shares[7],
            shares[8],
        ),
        "seq",
    )
    return (
        mixed,
        input_grad,
        totals[0],
        totals[1],
        totals[2],
        totals[3],
        totals[4],
        totals[5],
        totals[6],
        totals[7],
        totals[8],
    )


def solution(mesh):
    placed = (
        P("fsdp", "seq", None),
        P("fsdp"),
        P("fsdp"),
        P("fsdp", None),
        P(None, "fsdp"),
        P("fsdp"),
        P("fsdp"),
        P("fsdp"),
        P("fsdp"),
        P("fsdp"),
        P("fsdp", None),
        P("fsdp", "seq", None),
    )
    return jax.shard_map(
        per_device,
        mesh=mesh,
        in_specs=placed,
        out_specs=(
            P("fsdp", "seq", None),
            P("fsdp", "seq", None),
            P("fsdp"),
            P("fsdp", None),
            P(None, "fsdp"),
            P("fsdp"),
            P("fsdp"),
            P("fsdp"),
            P("fsdp"),
            P("fsdp"),
            P("fsdp", None),
        ),
        check_vma=False,
    )
```

profile of v0, /device:TPU:0, one launch (start us, length us, event | category | flops | bytes accessed | tf_op | source)
XLA Modules:
  0.0 1545.1 jit_solution(13398759697782761256)
XLA Ops:
  8.1 6.2 all-gather.3
  22.8 7.5 all-reduce.24
  32.0 105.5 %all-gather.10.cloned.1.call-done = bf16[1536,6448]{0,1:T(8,128)(2,1)} async-done(((bf16[384,6448]{0,1:T(8,128)(2,1)}), bf16[1536,6448]{0,1:T(8,128)(2,1)}) %all-gather.10.cloned.1.call-update) | async-done | bytes 19808272 | tf_op jit(solution)/shard_map/all_gather | solution.py:93
  137.4 9.9 fusion.6
  193.9 19.2 %all_gather.53 = f32[8,1,48]{2,1,0:T(1,128)} all-gather(f32[1,1,48]{2,1,0:T(1,128)} %get-tuple-element.423), channel_id=1, replica_groups=mesh['seq'=8,'fsdp'=4] {'seq'}, dimensions={0}, use_global_device_ids=true | all-gather | bytes 1728 | tf_op jit(solution)/shard_map/all_gather | solution.py:18
  218.5 131.1 %all-gather.14.cloned.1.call-done = f32[384,64,128]{2,1,0:T(8,128)} async-done(((f32[48,64,128]{2,1,0:T(8,128)}), f32[384,64,128]{2,1,0:T(8,128)}) %all-gather.14.cloned.1.call-update) | async-done | bytes 12582928 | tf_op jit(solution)/shard_map/all_gather | solution.py:18
  349.6 36.0 %while.30 = (s32[]{:T(128)}, f32[1,48,64,128]{3,2,1,0:T(8,128)}, s32[]{:T(128)}, f32[8,1,48]{2,1,0:T(1,128)}, f32[8,1,48,64,128]{4,3,2,1,0:T(8,128)}, /*index=5*/s32[]{:T(128)}, s32[]{:T(128)}) while((s32[]{:T(128)}, f32[1,48,64,128]{3,2,1,0:T(8,128)}, s32[]{:T(128)}, f32[8,1,48]{2,1,0:T(1,128)}, f32[8,1,48,64,128]{4,3,2,1,0:T(8,128)}, ...), condition=%wide.region_4.5_spmd.clone, body=%wide.region_3.4_spmd.clone.sunk | while | flops 1572868 | bytes 4719281 | solution.py:31
  388.6 9.6 fusion.34
  413.7 10.0 fusion.35
  423.7 5.9 multiply_reduce_fusion.5
  440.9 12.7 fusion.76
  457.7 14.9 fusion.8
  491.7 125.8 %all-gather.16.cloned.1.call-done = f32[384,64,128]{2,1,0:T(8,128)} async-done(((f32[48,64,128]{2,1,0:T(8,128)}), f32[384,64,128]{2,1,0:T(8,128)}) %all-gather.16.cloned.1.call-update) | async-done | bytes 12582928 | tf_op jit(solution)/shard_map/all_gather | solution.py:18
  617.5 38.9 %while.31 = (s32[]{:T(128)}, f32[1,48,64,128]{3,2,1,0:T(8,128)}, s32[]{:T(128)}, f32[8,1,48]{2,1,0:T(1,128)}, f32[8,1,48,64,128]{4,3,2,1,0:T(8,128)}, /*index=5*/s32[]{:T(128)}, s32[]{:T(128)}, s32[]{:T(128)}, s32[]{:T(128)}) while((s32[]{:T(128)}, f32[1,48,64,128]{3,2,1,0:T(8,128)}, s32[]{:T(128)}, f32[8,1,48]{2,1,0:T(1,128)}, ...), condition=%wide.region_8.9_spmd.clone, body=%wide.region_7.8_spmd.clone.sunk | while | flops 1572872 | bytes 4719343 | solution.py:31
  676.4 11.2 fusion.33
  712.6 18.4 %fusion.61 = f32[1536,6448]{0,1:T(8,128)} fusion(bf16[256,48]{1,0:T(8,128)(2,1)} %bitcast.336, bf16[256,3328]{1,0:T(8,128)(2,1)} %fusion.42, bf16[256,3072]{1,0:T(8,128)(2,1)} %get-tuple-element.412, bf16[1,256,1536]{2,1,0:T(8,128)(2,1)} %param.16, f32[1536]{0:T(1024)S(1)} %reshape.620, f32[256]{0:T(256)S(1)} %fusion.111), kind=kOutput, calls=%fused_computation.114 | convolution fusion | flops 5082390528 | bytes 43711488 | tf_op jit(solution)/shard_map/sqd,sqp->dp/dot_general | solution.py:179
  733.8 23.9 %reduce-scatter.8.cloned.1.call-done = f32[768,1536]{1,0:T(8,128)} async-done(((f32[3072,1536]{1,0:T(8,128)}), f32[768,1536]{1,0:T(8,128)}) %reduce-scatter.8.cloned.1.call-update) | async-done | bytes 4718608 | tf_op jit(solution)/shard_map/reduce_scatter | solution.py:196
  757.6 279.1 %reduce-scatter.6.cloned.1.call-done = f32[384,6448]{0,1:T(8,128)} async-done(((f32[1536,6448]{0,1:T(8,128)}), f32[384,6448]{0,1:T(8,128)}) %reduce-scatter.6.cloned.1.call-update) | async-done | bytes 9904144 | tf_op jit(solution)/shard_map/reduce_scatter | solution.py:189
  1040.0 7.5 fusion.39
  1047.6 10.0 fusion.44
  1057.6 12.3 all-reduce.23
  1073.3 39.6 %all-reduce.21 = (f32[384]{0:T(512)}, f32[4,832]{1,0:T(4,128)}, f32[832]{0:T(1024)}, f32[12]{0:T(128)}, f32[12]{0:T(128)}, /*index=5*/f32[12]{0:T(128)}, f32[768]{0:T(1024)}) all-reduce(f32[384]{0:T(512)S(1)} %dynamic-slice.5, f32[4,832]{1,0:T(4,128)S(1)} %copy.211, ...), channel_id=1, replica_groups=mesh['seq'=8,'fsdp'=4] {'seq'}, use_global_device_ids=true, to_apply=%region_21.22 | all-reduce | flops 5348 | bytes 42784 | tf_op jit(solution)/shard_map/psum | solution.py:198
  1112.9 414.5 %all-reduce.27.cloned.1.call-done = (f32[384,6448]{0,1:T(8,128)}, f32[768,1536]{1,0:T(8,128)}) async-done(((f32[384,6448]{0,1:T(8,128)}, f32[768,1536]{1,0:T(8,128)}), (f32[384,6448]{0,1:T(8,128)}, f32[768,1536]{1,0:T(8,128)})) %all-reduce.27.cloned.1.call-update) | async-done | bytes 14622736 | tf_op jit(solution)/shard_map/psum | solution.py:198
  1527.4 8.5 copy.231
  (294 shorter events, 241.7 us)
Async XLA Ops:
  7.2 12.7 copy-start.52
  7.2 14.6 copy-start.59
  7.2 14.8 copy-start.60
  7.2 15.1 copy-start.61
  7.2 15.3 copy-start.53
  7.3 24.4 %copy-start.11 = (bf16[1,256,1536]{2,1,0:T(8,128)(2,1)S(1)}, bf16[1,256,1536]{2,1,0:T(8,128)(2,1)}, u32[]{:S(2)}) copy-start(bf16[1,256,1536]{2,1,0:T(8,128)(2,1)} %param.16) | copy-start | bytes 2359300
  7.3 130.2 %all-gather.10.cloned.1.call-start = ((), (), s32[]{:S(2)}) async-start(), calls=%async_computation.3 | async-start | bytes 24760320 | tf_op jit(solution)/shard_map/all_gather | solution.py:93
  8.0 341.6 %all-gather.14.cloned.1.call-start = ((), (), s32[]{:S(2)}) async-start(), calls=%async_computation.7 | async-start | bytes 14155776 | tf_op jit(solution)/shard_map/all_gather | solution.py:18
  30.3 117.0 %copy-start.62 = (bf16[48]{0:T(256)(128)(2,1)}, bf16[48]{0:T(256)(128)(2,1)S(1)}, u32[]{:S(2)}) copy-start(bf16[48]{0:T(256)(128)(2,1)S(1)} %get-tuple-element.398) | copy-start | bytes 292
  30.9 125.8 %copy-start.40 = (f32[48]{0:T(128)}, f32[48]{0:T(128)S(1)}, u32[]{:S(2)}) copy-start(f32[48]{0:T(128)S(1)} %convert_element_type.95) | copy-start | bytes 580
  31.9 115.4 %copy-start.44 = (f32[256]{0:T(256)}, f32[256]{0:T(256)S(1)}, u32[]{:S(2)}) copy-start(f32[256]{0:T(256)S(1)} %fusion.46) | copy-start | bytes 3076
  31.9 115.4 %copy-start.55 = (f32[48]{0:T(128)}, f32[48]{0:T(128)S(1)}, u32[]{:S(2)}) copy-start(f32[48]{0:T(128)S(1)} %convert_exponential_fusion) | copy-start | bytes 580
  147.3 12.2 copy-start.10
  151.5 8.1 collective-permute-start
  174.5 239.2 %all-gather.12.cloned.1.call-start = ((), (), s32[]{:S(2)}) async-start(), calls=%async_computation.4 | async-start | bytes 11796480 | tf_op jit(solution)/shard_map/all_gather | solution.py:100
  175.2 442.3 %all-gather.16.cloned.1.call-start = ((), (), s32[]{:S(2)}) async-start(), calls=%async_computation.8 | async-start | bytes 14155776 | tf_op jit(solution)/shard_map/all_gather | solution.py:18
  440.9 316.7 %reduce-scatter.8.cloned.1.call-start = ((), (), s32[]{:S(2)}) async-start(), calls=%async_computation.6 | async-start | bytes 23592960 | tf_op jit(solution)/shard_map/reduce_scatter | solution.py:196
  453.7 583.1 %reduce-scatter.6.cloned.1.call-start = ((), (), s32[]{:S(2)}) async-start(), calls=%async_computation.5 | async-start | bytes 49520640 | tf_op jit(solution)/shard_map/reduce_scatter | solution.py:189
  704.4 6.0 collective-permute-start.1
  731.1 341.0 %reduce-scatter.10.cloned.1.call-start = ((), (), s32[]{:S(2)}) async-start(), calls=%async_computation.9 | async-start | bytes 2129920
  733.7 793.7 %all-reduce.27.cloned.1.call-start = ((), (), s32[]{:S(2)}) async-start(), calls=%async_computation.10 | async-start | bytes 29245440 | tf_op jit(solution)/shard_map/psum | solution.py:198
  1047.6 22.8 %copy-start.45 = (f32[256]{0:T(256)S(1)}, f32[256]{0:T(256)}, u32[]{:S(2)}) copy-start(f32[256]{0:T(256)} %copy-done.44) | copy-start | bytes 3076
  1047.6 22.8 %copy-start.13 = (bf16[1,256,1536]{2,1,0:T(8,128)(2,1)S(1)}, bf16[1,256,1536]{2,1,0:T(8,128)(2,1)}, u32[]{:S(2)}) copy-start(bf16[1,256,1536]{2,1,0:T(8,128)(2,1)} %param.16) | copy-start | bytes 2359300
  1047.6 22.8 %copy-start.20 = (bf16[1,256,1536]{2,1,0:T(8,128)(2,1)S(1)}, bf16[1,256,1536]{2,1,0:T(8,128)(2,1)}, u32[]{:S(2)}) copy-start(bf16[1,256,1536]{2,1,0:T(8,128)(2,1)} %param.27) | copy-start | bytes 2359300
  (51 other events, 259.4 us)
Sparse Core Ops, SparseCore 0:
  9.7 127.6 all-gather.9
  174.6 174.9 all-gather.13
  351.2 62.4 all-gather.11
  441.0 176.4 all-gather.15
  619.9 137.6 reduce-scatter.7
  760.3 276.4 reduce-scatter.5
  1039.9 29.6 reduce-scatter.9
  1074.5 452.8 all-reduce.26
where the time goes:
time: 1550 us
  waiting for transfers between devices  1090 us (70%)
  matrix products  135 us (9%)
  other arithmetic  113 us (7%)
  blocking collectives  95.4 us (6%)
  local copies, waits for them, and re-layouts  88.4 us (6%)
  between operations  20.1 us (1%)
    psum x1, waiting for transfers between devices, per_device(): lax.psum((shares[0], shares[1], shares[2], shares[3], shares[4], shares[5...  415 us
    reduce_scatter x1, waiting for transfers between devices, per_device(): lax.psum_scatter(grad_in_w, 'fsdp', scatter_dimension=0, tiled=True)  279 us
    all_gather x2, waiting for transfers between devices, carried_in(): everything = jax.tree.map(lambda part: lax.all_gather(part, axis), value)  257 us
    all_gather x1, waiting for transfers between devices, per_device(): lax.all_gather(in_weight, 'fsdp', axis=0, tiled=True)  105 us
    select_n x16, other arithmetic, lap(): return jax.tree.map(lambda a, b: jnp.where(reached, a, b), new, before)  56.7 us
    psum x1, blocking collectives, per_device(): lax.psum((shares[0], shares[1], shares[2], shares[3], shares[4], shares[5...  39.6 us
    dot_general x3, matrix products, local_scan(): local_out = jnp.einsum('stuh,suhp->sthp', mixing, values, precision=triple)  35.7 us
  transfers between devices with their start and end apart: 10, of which 8 were waited for; matrix products, arithmetic and copies ran while one was open for 17% of the time, Pallas kernels for 0%

commit v1 on v0

--- a/solution.py
+++ b/solution.py
@@ -5,6 +5,20 @@
 
 epsilon = 1e-05
 triple = lax.Precision.HIGH
+
+
+def point_block_over_axis(frame):
+    piece_next = lax.axis_size("fsdp")
+    frame_out = lax.axis_index("fsdp")
+    a_next, carry_out = (piece_next, frame_out)
+    small, outer = (frame, 1)
+    while outer < a_next:
+        back = lax.ppermute(small, "fsdp", [(d, d ^ outer) for d in range(a_next)])
+        f_now = jnp.concatenate([small, back], axis=0)
+        after = jnp.concatenate([back, small], axis=0)
+        small = jnp.where(carry_out & outer == 0, f_now, after)
+        outer = 2 * outer
+    return small
 
 
 def from_behind(value, axis, by):
@@ -90,7 +104,7 @@
 ):
     gathered = (
         lax.all_gather(norm_gain, "fsdp", axis=0, tiled=True),
-        lax.all_gather(in_weight, "fsdp", axis=0, tiled=True),
+        point_block_over_axis(in_weight),
         lax.all_gather(conv_weight, "fsdp", axis=1, tiled=True),
         lax.all_gather(conv_bias, "fsdp", axis=0, tiled=True),
         lax.all_gather(dt_bias, "fsdp", axis=0, tiled=True),

time: 1550 us -> 1820 us (1.17)
  blocking collectives: 95.4 us -> 302 us
  waiting for transfers between devices: 1090 us -> 1110 us
    all_gather x1, blocking collectives: 6.22 us -> 214 us  [per_device(): lax.all_gather(conv_weight, 'fsdp', axis=1, tiled=True)]
  transfers between devices with their start and end apart: 10 -> 12, of which waited for: 8 -> 10; matrix products, arithmetic and copies ran while one was open for 17% -> 15% of each run, Pallas kernels for 0% -> 0%
where the time goes in v1:
time: 1820 us; the launch traced here: 1810 us
  waiting for transfers between devices  1110 us (61%)
  blocking collectives  302 us (17%)
  matrix products  146 us (8%)
  other arithmetic  126 us (7%)
  local copies, waits for them, and re-layouts  87.8 us (5%)
  between operations  20.2 us (1%)
    psum x1, waiting for transfers between devices, per_device(): lax.psum((shares[0], shares[1], shares[2], shares[3], shares[4], shares[5...  418 us
    reduce_scatter x1, waiting for transfers between devices, per_device(): lax.psum_scatter(grad_in_w, 'fsdp', scatter_dimension=0, tiled=True)  279 us
    all_gather x2, waiting for transfers between devices, carried_in(): everything = jax.tree.map(lambda part: lax.all_gather(part, axis), value)  249 us
    all_gather x1, blocking collectives, per_device(): lax.all_gather(conv_weight, 'fsdp', axis=1, tiled=True)  214 us
    all_gather x1, waiting for transfers between devices, per_device(): lax.all_gather(in_weight, 'fsdp', axis=0, tiled=True)  116 us
    select_n x16, other arithmetic, lap(): return jax.tree.map(lambda a, b: jnp.where(reached, a, b), new, before)  56.9 us
    psum x1, blocking collectives, per_device(): lax.psum((shares[0], shares[1], shares[2], shares[3], shares[4], shares[5...  39.2 us
  transfers between devices with their start and end apart: 12, of which 10 were waited for; matrix products, arithmetic and copies ran while one was open for 15% of the time, Pallas kernels for 0%

profile of v1, /device:TPU:0, one launch (start us, length us, event | category | flops | bytes accessed | tf_op | source)
XLA Modules:
  0.0 1806.6 jit_solution(8370006020926846153)
XLA Ops:
  7.8 8.2 collective-permute-done
  16.0 13.1 maximum_select_fusion.2
  32.0 214.5 %all-gather.3 = bf16[4,832,4]{1,2,0:T(4,128)(2,1)S(1)} all-gather(bf16[1,832,4]{1,2,0:T(4,128)(2,1)S(1)} %bitcast.342), channel_id=1, replica_groups=mesh['seq'=8,'fsdp'=4] {'fsdp'}, dimensions={0}, use_global_device_ids=true | all-gather | bytes 33280 | tf_op jit(solution)/shard_map/all_gather | solution.py:108
  263.9 18.2 %fusion.14 = bf16[1,256,6448]{2,1,0:T(8,128)(2,1)S(1)} fusion(bf16[768,6448]{0,1:T(8,128)(2,1)} %collective-permute-done.1, bf16[768,6448]{0,1:T(8,128)(2,1)} %maximum_select_fusion.2, pred[]{:T(512)S(6)} %eq.14, bf16[1,256,1536]{2,1,0:T(8,128)(2,1)} %param.16, f32[1536]{0:T(1024)S(1)} %reshape.620, f32[256]{0:T(256)S(1)} %fusion.119), kind=kOutput, calls=%fused_computation.26 | convolution fusion | flops 5163274240 | bytes 23903232 | tf_op jit(solution)/shard_map/sqd,dp->sqp/dot_general | solution.py:133
  328.8 19.5 %all_gather.51 = f32[8,1,48]{2,1,0:T(1,128)} all-gather(f32[1,1,48]{2,1,0:T(1,128)} %get-tuple-element.423), channel_id=1, replica_groups=mesh['seq'=8,'fsdp'=4] {'seq'}, dimensions={0}, use_global_device_ids=true | all-gather | bytes 1728 | tf_op jit(solution)/shard_map/all_gather | solution.py:32
  353.6 131.1 %all-gather.14.cloned.1.call-done = f32[384,64,128]{2,1,0:T(8,128)} async-done(((f32[48,64,128]{2,1,0:T(8,128)}), f32[384,64,128]{2,1,0:T(8,128)}) %all-gather.14.cloned.1.call-update) | async-done | bytes 12582928 | tf_op jit(solution)/shard_map/all_gather | solution.py:32
  484.8 36.0 %while.30 = (s32[]{:T(128)}, f32[1,48,64,128]{3,2,1,0:T(8,128)}, s32[]{:T(128)}, f32[8,1,48]{2,1,0:T(1,128)}, f32[8,1,48,64,128]{4,3,2,1,0:T(8,128)}, /*index=5*/s32[]{:T(128)}, s32[]{:T(128)}) while((s32[]{:T(128)}, f32[1,48,64,128]{3,2,1,0:T(8,128)}, s32[]{:T(128)}, f32[8,1,48]{2,1,0:T(1,128)}, f32[8,1,48,64,128]{4,3,2,1,0:T(8,128)}, ...), condition=%wide.region_4.5_spmd.clone, body=%wide.region_3.4_spmd.clone.sunk | while | flops 1572868 | bytes 4719281 | solution.py:45
  523.8 9.6 fusion.42
  548.8 10.1 fusion.43
  576.2 12.7 fusion.84
  588.9 8.7 reduce-scatter.6.cloned.1.call-start
  601.3 14.9 fusion.16
  635.3 117.4 %all-gather.16.cloned.1.call-done = f32[384,64,128]{2,1,0:T(8,128)} async-done(((f32[48,64,128]{2,1,0:T(8,128)}), f32[384,64,128]{2,1,0:T(8,128)}) %all-gather.16.cloned.1.call-update) | async-done | bytes 12582928 | tf_op jit(solution)/shard_map/all_gather | solution.py:32
  752.7 39.0 %while.31 = (s32[]{:T(128)}, f32[1,48,64,128]{3,2,1,0:T(8,128)}, s32[]{:T(128)}, f32[8,1,48]{2,1,0:T(1,128)}, f32[8,1,48,64,128]{4,3,2,1,0:T(8,128)}, /*index=5*/s32[]{:T(128)}, s32[]{:T(128)}, s32[]{:T(128)}, s32[]{:T(128)}) while((s32[]{:T(128)}, f32[1,48,64,128]{3,2,1,0:T(8,128)}, s32[]{:T(128)}, f32[8,1,48]{2,1,0:T(1,128)}, ...), condition=%wide.region_8.9_spmd.clone, body=%wide.region_7.8_spmd.clone.sunk | while | flops 1572872 | bytes 4719343 | solution.py:45
  811.8 11.0 fusion.41
  847.8 18.5 %fusion.69 = f32[1536,6448]{0,1:T(8,128)} fusion(bf16[256,48]{1,0:T(8,128)(2,1)} %bitcast.335, bf16[256,3328]{1,0:T(8,128)(2,1)} %fusion.50, bf16[256,3072]{1,0:T(8,128)(2,1)} %get-tuple-element.412, bf16[1,256,1536]{2,1,0:T(8,128)(2,1)} %param.16, f32[1536]{0:T(1024)S(1)} %reshape.620, f32[256]{0:T(256)S(1)} %fusion.119), kind=kOutput, calls=%fused_computation.123 | convolution fusion | flops 5082390528 | bytes 43711488 | tf_op jit(solution)/shard_map/sqd,sqp->dp/dot_general | solution.py:193
  869.0 23.8 %reduce-scatter.8.cloned.1.call-done = f32[768,1536]{1,0:T(8,128)} async-done(((f32[3072,1536]{1,0:T(8,128)}), f32[768,1536]{1,0:T(8,128)}) %reduce-scatter.8.cloned.1.call-update) | async-done | bytes 4718608 | tf_op jit(solution)/shard_map/reduce_scatter | solution.py:210
  892.8 279.1 %reduce-scatter.6.cloned.1.call-done = f32[384,6448]{0,1:T(8,128)} async-done(((f32[1536,6448]{0,1:T(8,128)}), f32[384,6448]{0,1:T(8,128)}) %reduce-scatter.6.cloned.1.call-update) | async-done | bytes 9904144 | tf_op jit(solution)/shard_map/reduce_scatter | solution.py:203
  1182.6 115.7 %all-gather.12.cloned.1.call-done = bf16[1536,6448]{0,1:T(8,128)(2,1)} async-done(((bf16[384,6448]{0,1:T(8,128)(2,1)}), bf16[1536,6448]{0,1:T(8,128)(2,1)}) %all-gather.12.cloned.1.call-update) | async-done | bytes 19808272 | tf_op jit(solution)/shard_map/all_gather | solution.py:160
  1298.3 13.3 fusion.52
  1311.6 11.3 all-reduce.23
  1331.9 39.2 %all-reduce.21 = (f32[384]{0:T(512)}, f32[4,832]{1,0:T(4,128)}, f32[832]{0:T(1024)}, f32[12]{0:T(128)}, f32[12]{0:T(128)}, /*index=5*/f32[12]{0:T(128)}, f32[768]{0:T(1024)}) all-reduce(f32[384]{0:T(512)S(1)} %dynamic-slice.5, f32[4,832]{1,0:T(4,128)S(1)} %copy.211, ...), channel_id=1, replica_groups=mesh['seq'=8,'fsdp'=4] {'seq'}, use_global_device_ids=true, to_apply=%region_21.22 | all-reduce | flops 5348 | bytes 42784 | tf_op jit(solution)/shard_map/psum | solution.py:212
  1371.1 417.6 %all-reduce.27.cloned.1.call-done = (f32[384,6448]{0,1:T(8,128)}, f32[768,1536]{1,0:T(8,128)}) async-done(((f32[384,6448]{0,1:T(8,128)}, f32[768,1536]{1,0:T(8,128)}), (f32[384,6448]{0,1:T(8,128)}, f32[768,1536]{1,0:T(8,128)})) %all-reduce.27.cloned.1.call-update) | async-done | bytes 14622736 | tf_op jit(solution)/shard_map/psum | solution.py:212
  1788.7 8.5 copy.231
  (293 shorter events, 270.6 us)
Async XLA Ops:
  7.2 477.6 %all-gather.14.cloned.1.call-start = ((), (), s32[]{:S(2)}) async-start(), calls=%async_computation.7 | async-start | bytes 14155776 | tf_op jit(solution)/shard_map/all_gather | solution.py:32
  7.2 8.7 collective-permute-start
  7.7 238.9 %copy-start.54 = (bf16[384]{0:T(512)(128)(2,1)S(1)}, bf16[384]{0:T(512)(128)(2,1)}, u32[]{:S(2)}) copy-start(bf16[384]{0:T(512)(128)(2,1)} %param.18) | copy-start | bytes 2308
  7.7 244.1 %copy-start.49 = (u32[32]{0:T(128)S(1)}, u32[32]{0:T(128)}, u32[]{:S(2)}) copy-start(u32[32]{0:T(128)} %constant.145) | copy-start | bytes 388
  7.7 246.0 %copy-start.56 = (bf16[12]{0:T(256)(128)(2,1)S(1)}, bf16[12]{0:T(256)(128)(2,1)}, u32[]{:S(2)}) copy-start(bf16[12]{0:T(256)(128)(2,1)} %param.23) | copy-start | bytes 76
  7.8 246.3 %copy-start.57 = (bf16[12]{0:T(256)(128)(2,1)S(1)}, bf16[12]{0:T(256)(128)(2,1)}, u32[]{:S(2)}) copy-start(bf16[12]{0:T(256)(128)(2,1)} %param.22) | copy-start | bytes 76
  7.8 246.5 %copy-start.58 = (bf16[12]{0:T(256)(128)(2,1)S(1)}, bf16[12]{0:T(256)(128)(2,1)}, u32[]{:S(2)}) copy-start(bf16[12]{0:T(256)(128)(2,1)} %param.24) | copy-start | bytes 76
  7.8 246.7 %copy-start.50 = (bf16[832]{0:T(1024)(128)(2,1)S(1)}, bf16[832]{0:T(1024)(128)(2,1)}, u32[]{:S(2)}) copy-start(bf16[832]{0:T(1024)(128)(2,1)} %param.21) | copy-start | bytes 4996
  7.8 255.9 %copy-start.11 = (bf16[1,256,1536]{2,1,0:T(8,128)(2,1)S(1)}, bf16[1,256,1536]{2,1,0:T(8,128)(2,1)}, u32[]{:S(2)}) copy-start(bf16[1,256,1536]{2,1,0:T(8,128)(2,1)} %param.16) | copy-start | bytes 2359300
  29.1 234.8 %collective-permute-start.1 = (bf16[768,6448]{0,1:T(8,128)(2,1)}, bf16[768,6448]{0,1:T(8,128)(2,1)}, u32[]{:S(2)}, u32[]{:S(2)}) collective-permute-start(bf16[768,6448]{0,1:T(8,128)(2,1)} %maximum_select_fusion.2), channel_id=1, source_target_pairs={{0,2},{1,3},{2,0},{3,1},{4,6},{5,7},{6,4},{7,5},{8,10},{9,11},{10,... | collective-permute-start | bytes 29712392 | tf_op jit(solution)/shard_map/ppermute | solution.py:16
  286.3 8.1 collective-permute-start.2
  309.4 239.4 %all-gather.10.cloned.1.call-start = ((), (), s32[]{:S(2)}) async-start(), calls=%async_computation.3 | async-start | bytes 11796480 | tf_op jit(solution)/shard_map/all_gather | solution.py:114
  310.1 442.6 %all-gather.16.cloned.1.call-start = ((), (), s32[]{:S(2)}) async-start(), calls=%async_computation.8 | async-start | bytes 14155776 | tf_op jit(solution)/shard_map/all_gather | solution.py:32
  576.1 316.7 %reduce-scatter.8.cloned.1.call-start = ((), (), s32[]{:S(2)}) async-start(), calls=%async_computation.6 | async-start | bytes 23592960 | tf_op jit(solution)/shard_map/reduce_scatter | solution.py:210
  588.9 583.0 %reduce-scatter.6.cloned.1.call-start = ((), (), s32[]{:S(2)}) async-start(), calls=%async_computation.5 | async-start | bytes 49520640 | tf_op jit(solution)/shard_map/reduce_scatter | solution.py:203
  839.5 6.0 collective-permute-start.3
  866.4 431.9 %all-gather.12.cloned.1.call-start = ((), (), s32[]{:S(2)}) async-start(), calls=%async_computation.4 | async-start | bytes 24760320 | tf_op jit(solution)/shard_map/all_gather | solution.py:160
  867.0 463.7 %reduce-scatter.10.cloned.1.call-start = ((), (), s32[]{:S(2)}) async-start(), calls=%async_computation.9 | async-start | bytes 2129920
  869.0 919.7 %all-reduce.27.cloned.1.call-start = ((), (), s32[]{:S(2)}) async-start(), calls=%async_computation.10 | async-start | bytes 29245440 | tf_op jit(solution)/shard_map/psum | solution.py:212
  1182.6 129.0 %copy-start.29 = (f32[3328]{0:T(1024)S(1)}, f32[3328]{0:T(1024)}, u32[]{:S(2)}) copy-start(f32[3328]{0:T(1024)} %get-tuple-element.355) | copy-start | bytes 39940
  1182.6 129.0 %copy-start.39 = (f32[3072]{0:T(1024)S(1)}, f32[3072]{0:T(1024)}, u32[]{:S(2)}) copy-start(f32[3072]{0:T(1024)} %get-tuple-element.353) | copy-start | bytes 36868
  1182.6 140.7 %copy-start.42 = (f32[256]{0:T(256)S(1)}, f32[256]{0:T(256)}, u32[]{:S(2)}) copy-start(f32[256]{0:T(256)} %copy-done.41) | copy-start | bytes 3076
  1182.6 140.7 %copy-start.12 = (bf16[1,256,1536]{2,1,0:T(8,128)(2,1)S(1)}, bf16[1,256,1536]{2,1,0:T(8,128)(2,1)}, u32[]{:S(2)}) copy-start(bf16[1,256,1536]{2,1,0:T(8,128)(2,1)} %param.16) | copy-start | bytes 2359300
  1182.6 140.7 %copy-start.17 = (bf16[1,256,1536]{2,1,0:T(8,128)(2,1)S(1)}, bf16[1,256,1536]{2,1,0:T(8,128)(2,1)}, u32[]{:S(2)}) copy-start(bf16[1,256,1536]{2,1,0:T(8,128)(2,1)} %param.27) | copy-start | bytes 2359300
  (50 other events, 564.6 us)
Sparse Core Ops, SparseCore 0:
  309.5 175.2 all-gather.13
  486.3 62.4 all-gather.9
  576.2 176.4 all-gather.15
  755.1 137.6 reduce-scatter.7
  895.5 276.4 reduce-scatter.5
  1173.4 124.8 all-gather.11
  1301.4 29.2 reduce-scatter.9
  1335.6 453.0 all-reduce.26
